TPU v7x, 32 devices: a whole 2x2x4 slice. The times are simulated.
32 devices in a mesh: gx: 4 (over x, core), gy: 8 (over z, y).
Axes of the slice: x: 2, y: 2, z: 4, core: 2. Of those that a mesh axis runs over, the one named last changes fastest.
Arguments:
- right_side: bfloat16 [4, 8, 8, 625, 256], P('gx', 'gy'), may hold values from -6 to 6
- inverse_blocks: bfloat16 [4, 8, 8, 625, 625], P('gx', 'gy'), may hold values from -0.2 to 0.8
- lift_matrix: bfloat16 [625, 375], replicated, may hold values from -2 to 2
- plane_order: int32 [4, 8, 8], P('gx', 'gy'), may hold values from 0 to 7, each once within a row
- face_orient: int32 [4, 8, 8, 3], P('gx', 'gy'), may hold values from 0 to 7
Outputs:
- solution: bfloat16 [4, 8, 8, 625, 256], P('gx', 'gy')
Inputs may be any that keep to these rules, and one draw needn't show every extreme that they name: `plane_order`: each slab's row lists the storage slots of its 8 elements from lowest to highest z, each slot once. `face_orient`: any of the eight orientations of a square face.
All inputs are finite; a program needn't handle non-finite values.
Results may differ from a plain program's by a relative error of at most 0.025.
Values may be sent and summed in bfloat16 or wider, within the bound.
A program may use at most 64 MiB of HBM per device.

v0:
```python
import functools

import jax
import jax.numpy as jnp
import numpy as np
from jax import lax
from jax.experimental import pallas as pl
from jax.experimental.pallas import tpu as pltpu
from jax.sharding import PartitionSpec as P

VARS = 5
NODES = 5
SQUARE = NODES * NODES
FACE = VARS * SQUARE
BLOCK = FACE * NODES
LANE = 128
CHUNKS = 1
MESH = pl.DeviceIdType.MESH


def orient_table():
    table = np.zeros((8, LANE, LANE), np.float32)
    for orient in range(8):
        for variable in range(VARS):
            for first in range(NODES):
                for second in range(NODES):
                    p, q = (second, first) if orient & 1 else (first, second)
                    if orient & 2:
                        p = NODES - 1 - p
                    if orient & 4:
                        q = NODES - 1 - q
                    target = variable * SQUARE + first * NODES + second
                    table[orient, target, variable * SQUARE + p * NODES + q] = 1.0
    return table


def dot(a, b):
    return jnp.dot(a, b, preferred_element_type=jnp.float32)


def row_chunks(block):
    return [(start, min(LANE, block - start)) for start in range(0, block, LANE)]


def sweep_kernel(
    order, orient, table_hbm, lift_hbm, rhs_hbm, inv_hbm, sol,
    table, lift, raw_r, raw_b, stage, rhs, inv, padded, turned, wide, part, picked, trace_m, trace_r,
    inc, out, load_sem, r_sem, b_sem, x_send, y_send, x_recv, y_recv,
):
    planes, block, columns = rhs.shape
    width = columns // CHUNKS
    two, three = 2 * LANE, 3 * LANE
    chunks = row_chunks(block)
    tiles = [(t, min(LANE, block - t)) for t in range(0, block, LANE)]
    count_x, count_y = lax.axis_size("gx"), lax.axis_size("gy")
    me_x, me_y = lax.axis_index("gx"), lax.axis_index("gy")
    has_left, has_right = me_x > 0, me_x < count_x - 1
    has_below, has_above = me_y > 0, me_y < count_y - 1

    loads = [
        pltpu.make_async_copy(source, target, load_sem.at[i])
        for i, (source, target) in enumerate([(lift_hbm, lift), (table_hbm, table)])
    ]
    for load in loads:
        load.start()

    def fetch(i, start, size):
        rows = pl.ds(start, size)
        return (
            pltpu.make_async_copy(rhs_hbm.at[rows], raw_r.at[rows], r_sem.at[i]),
            pltpu.make_async_copy(inv_hbm.at[rows], raw_b.at[rows], b_sem.at[i]),
        )

    whole = block // LANE
    depth = min(2, len(chunks))
    for i, (start, size) in list(enumerate(chunks))[:depth]:
        for copy in fetch(i, start, size):
            copy.start()

    barrier = pltpu.get_barrier_semaphore()
    for present, x, y in (
        (has_left, me_x - 1, me_y),
        (has_right, me_x + 1, me_y),
        (has_below, me_x, me_y - 1),
        (has_above, me_x, me_y + 1),
    ):
        @pl.when(present)
        def _():
            pl.semaphore_signal(barrier, inc=1, device_id=(x, y), device_id_type=MESH)

    part[...] = jnp.zeros_like(part)
    out[0] = jnp.zeros(out.shape[1:], out.dtype)

    @pl.when(me_x == 0)
    def _():
        inc[:, :, :LANE, :] = jnp.zeros((planes, CHUNKS, LANE, width), inc.dtype)

    @pl.when(me_y == 0)
    def _():
        inc[:, :, LANE:, :] = jnp.zeros((planes, CHUNKS, LANE, width), inc.dtype)

    row = lax.broadcasted_iota(jnp.int32, (3 * FACE, three), 0)
    col = lax.broadcasted_iota(jnp.int32, (3 * FACE, three), 1)
    face = jnp.where(col >= two, 2, jnp.where(col >= LANE, 1, 0))
    inside = col - face * LANE
    spread = ((inside < FACE) & (row == face * FACE + inside)).astype(jnp.float32).astype(jnp.bfloat16)
    loads[0].wait()
    padded[...] = lax.dot_general(
        lift[...], spread, (((0,), (0,)), ((), ())), preferred_element_type=jnp.float32
    ).astype(jnp.bfloat16)
    loads[1].wait()

    def split(raw, into, rows, size, lanes, t):
        mixed = raw[rows, :, lanes].astype(jnp.float32)
        wide_lanes = mixed.shape[-1]
        stage[t, : size * planes, :wide_lanes] = mixed.reshape(size * planes, wide_lanes)
        for s in range(planes):
            apart = stage[t, pl.ds(s, size, stride=planes), :]
            into[s, rows, lanes] = apart[:, :wide_lanes].astype(jnp.bfloat16)

    def arrange(i, start, size):
        for copy in fetch(i, start, size):
            copy.wait()
        if size == LANE:
            @pl.when(i + depth < whole)
            def _():
                for copy in fetch(i + depth, pl.multiple_of(start + depth * LANE, LANE), LANE):
                    copy.start()

            if whole < len(chunks):
                @pl.when(i + depth == whole)
                def _():
                    for copy in fetch(whole, *chunks[whole]):
                        copy.start()

        rows = pl.ds(start, size)
        for t, (first, wide_lanes) in enumerate(tiles):
            split(raw_b, inv, rows, size, slice(first, first + wide_lanes), t)
        for t in range(columns // LANE):
            split(raw_r, rhs, rows, size, slice(t * LANE, (t + 1) * LANE), len(tiles) + t)

    def arrange_full(i, carry):
        arrange(i, pl.multiple_of(i * LANE, LANE), LANE)
        return carry

    lax.fori_loop(0, whole, arrange_full, 0)
    for i, (start, size) in list(enumerate(chunks))[whole:]:
        arrange(i, start, size)

    def pick(source, put):
        for v in range(VARS):
            put(v * SQUARE, source[pl.ds(v * FACE + FACE - SQUARE, SQUARE), :])
        for v in range(VARS * NODES):
            put(LANE + v * NODES, source[pl.ds(v * SQUARE + SQUARE - NODES, NODES), :])
        put(two, source[pl.ds(NODES - 1, FACE, stride=NODES), :])

    def prepare(k):
        slot = order[k]
        for t, (first, wide_lanes) in enumerate(tiles):
            wide[t, :, :wide_lanes] = inv[slot, :, first : first + wide_lanes].astype(jnp.float32)

            def put(start, rows):
                part[t, pl.ds(start, rows.shape[0]), :] = rows

            pick(wide.at[t], put)
            picked[:, first : first + wide_lanes] = part[t, :, :wide_lanes].astype(jnp.bfloat16)
        moved = dot(picked[...], padded[...]).astype(jnp.bfloat16)
        for d in range(3):
            tile = slice(d * LANE, (d + 1) * LANE)
            trace_m[k, :, tile] = dot(moved[:, tile], table[orient[d, 0, slot]]).astype(jnp.bfloat16)
        plain = dot(picked[...], rhs[slot])
        for c in range(CHUNKS):
            trace_r[k, c] = plain[:, c * width : (c + 1) * width]

    def hop(k, c, axis):
        rows = pl.ds(axis * LANE, LANE)
        send, recv = ((x_send, x_recv), (y_send, y_recv))[axis]
        return pltpu.make_async_remote_copy(
            src_ref=out.at[k + 1, c, rows, :],
            dst_ref=inc.at[k, c, rows, :],
            send_sem=send.at[k, c],
            recv_sem=recv.at[k, c],
            device_id=((me_x + 1, me_y), (me_x, me_y + 1))[axis],
            device_id_type=MESH,
        )

    def advance(k, c):
        started = trace_r[k, c] - dot(trace_m[k, :, two:], out[k, c, two:, :])

        @pl.when(has_left)
        def _():
            hop(k, c, 0).wait_recv()

        @pl.when(has_below)
        def _():
            hop(k, c, 1).wait_recv()

        arrived = inc[k, c]
        ahead_rows = (started[:two] - dot(trace_m[k, :two, :two], arrived)).astype(jnp.bfloat16)
        out[k + 1, c, LANE:two, :] = ahead_rows[LANE:]

        @pl.when(has_above)
        def _():
            hop(k, c, 1).start()

        out[k + 1, c, :LANE, :] = ahead_rows[:LANE]

        @pl.when(has_right)
        def _():
            hop(k, c, 0).start()

        out[k + 1, c, two:, :] = (started[two:] - dot(trace_m[k, two:, :two], arrived)).astype(jnp.bfloat16)

    def finish(k):
        slot = order[k]
        faces = [[inc[k, c, d * LANE : (d + 1) * LANE, :] for c in range(CHUNKS)] for d in range(2)]
        faces.append([out[k, c, two:, :] for c in range(CHUNKS)])
        for d in range(3):
            face = jnp.concatenate(faces[d], axis=-1)
            turned[d * LANE : (d + 1) * LANE, :] = dot(table[orient[d, 0, slot]], face).astype(jnp.bfloat16)
        lifted = dot(padded[...], turned[...])
        source = (rhs[slot].astype(jnp.float32) - lifted).astype(jnp.bfloat16)
        sol[k] = dot(inv[slot], source).astype(jnp.bfloat16)

    distance = me_x + me_y
    lead = jnp.minimum(1 + 2 * distance, planes)
    near = distance * 2 <= count_x + count_y - 2

    def ahead(k, carry):
        prepare(k)
        return carry

    lax.fori_loop(0, lead, ahead, 0)

    neighbours = sum(p.astype(jnp.int32) for p in (has_left, has_right, has_below, has_above))
    pl.semaphore_wait(barrier, neighbours)

    def step(k, carry):
        for c in range(CHUNKS):
            advance(k, c)

        @pl.when(k + lead < planes)
        def _():
            prepare(k + lead)

        @pl.when(jnp.logical_not(near))
        def _():
            finish(k)

        return carry

    lax.fori_loop(0, planes, step, 0)

    @pl.when(near)
    def _():
        def late(k, carry):
            finish(k)
            return carry

        lax.fori_loop(0, planes, late, 0)

    def drain(k, carry):
        for c in range(CHUNKS):
            @pl.when(has_right)
            def _():
                hop(k, c, 0).wait_send()

            @pl.when(has_above)
            def _():
                hop(k, c, 1).wait_send()
        return carry

    lax.fori_loop(0, planes, drain, 0)


def place_kernel(order, sol, out, stage, ready, sems):
    planes, block, columns = sol.shape
    chunks = row_chunks(block)
    whole = block // LANE

    def put(i, start, size):
        rows = pl.ds(start, size)
        return pltpu.make_async_copy(ready.at[rows], out.at[rows], sems.at[i])

    def place(i, start, size):
        rows = pl.ds(start, size)
        for t in range(columns // LANE):
            lanes = slice(t * LANE, (t + 1) * LANE)
            for k in range(planes):
                stage[t, pl.ds(order[k], size, stride=planes), :] = sol[k, rows, lanes].astype(jnp.float32)
            ready[rows, :, lanes] = (
                stage[t, : size * planes, :].reshape(size, planes, LANE).astype(jnp.bfloat16)
            )
        put(i, start, size).start()

    def place_full(i, carry):
        place(i, pl.multiple_of(i * LANE, LANE), LANE)
        return carry

    lax.fori_loop(0, whole, place_full, 0)
    for i, (start, size) in list(enumerate(chunks))[whole:]:
        place(i, start, size)
    for i, (start, size) in enumerate(chunks):
        put(i, start, size).wait()


def on_device(right_side, inverse_blocks, lift_matrix, plane_order, face_orient):
    rhs = jnp.transpose(right_side, (0, 1, 3, 2, 4))[0, 0]
    inv = jnp.transpose(inverse_blocks, (0, 1, 3, 2, 4))[0, 0]
    order = plane_order[0, 0]
    orient = jnp.transpose(face_orient, (0, 3, 1, 2))[0]
    block, planes, columns = rhs.shape
    tiles = pl.cdiv(block, LANE)
    chunks = len(row_chunks(block))
    width = columns // CHUNKS
    two, three = 2 * LANE, 3 * LANE
    bf16, f32 = jnp.bfloat16, jnp.float32
    table = jnp.asarray(orient_table(), bf16)
    lift = lift_matrix.T
    smem = pl.BlockSpec(memory_space=pltpu.SMEM)
    vmem = pl.BlockSpec(memory_space=pltpu.VMEM)
    anywhere = pl.BlockSpec(memory_space=pl.ANY)
    sol = pl.pallas_call(
        sweep_kernel,
        out_shape=pltpu.VMEM((planes, block, columns), bf16),
        in_specs=[smem, smem] + [anywhere] * 4,
        out_specs=vmem,
        scratch_shapes=[
            pltpu.VMEM(table.shape, bf16),
            pltpu.VMEM(lift.shape, bf16),
            pltpu.VMEM(rhs.shape, bf16),
            pltpu.VMEM(inv.shape, bf16),
            pltpu.VMEM((tiles + columns // LANE, LANE * planes, LANE), f32),
            pltpu.VMEM((planes, block, columns), bf16),
            pltpu.VMEM((planes, block, block), bf16),
            pltpu.VMEM((block, three), bf16),
            pltpu.VMEM((three, columns), bf16),
            pltpu.VMEM((tiles, block, LANE), f32),
            pltpu.VMEM((tiles, three, LANE), f32),
            pltpu.VMEM((three, block), bf16),
            pltpu.VMEM((planes, three, three), bf16),
            pltpu.VMEM((planes, CHUNKS, three, width), f32),
            pltpu.VMEM((planes, CHUNKS, two, width), bf16),
            pltpu.VMEM((planes + 1, CHUNKS, three, width), bf16),
            pltpu.SemaphoreType.DMA((2,)),
            pltpu.SemaphoreType.DMA((chunks,)),
            pltpu.SemaphoreType.DMA((chunks,)),
            pltpu.SemaphoreType.DMA((planes, CHUNKS)),
            pltpu.SemaphoreType.DMA((planes, CHUNKS)),
            pltpu.SemaphoreType.DMA((planes, CHUNKS)),
            pltpu.SemaphoreType.DMA((planes, CHUNKS)),
        ],
        compiler_params=pltpu.CompilerParams(
            collective_id=0, has_side_effects=True, vmem_limit_bytes=60 * 1024 * 1024
        ),
    )(order, orient, table, lift, rhs, inv)
    result = pl.pallas_call(
        place_kernel,
        out_shape=jax.ShapeDtypeStruct(rhs.shape, bf16),
        in_specs=[smem, vmem],
        out_specs=anywhere,
        scratch_shapes=[
            pltpu.VMEM((columns // LANE, LANE * planes, LANE), f32),
            pltpu.VMEM(rhs.shape, bf16),
            pltpu.SemaphoreType.DMA((chunks,)),
        ],
        compiler_params=pltpu.CompilerParams(vmem_limit_bytes=16 * 1024 * 1024),
    )(order, sol)
    return jnp.transpose(result[None, None], (0, 1, 3, 2, 4))


def solution(mesh):
    placed = (
        P("gx", "gy", None, None, None),
        P("gx", "gy", None, None, None),
        P(),
        P("gx", "gy", None),
        P("gx", "gy", None, None),
    )
    return jax.shard_map(
        on_device,
        mesh=mesh,
        in_specs=placed,
        out_specs=P("gx", "gy", None, None, None),
        check_vma=False,
    )
```

profile of v0, /device:TPU:31, one launch (start us, length us, event | category | flops | bytes accessed | tf_op | source)
XLA Modules:
  0.0 53.7 jit_solution(4550880114060611025)
XLA Ops:
  0.0 0.0 copy-start
  0.0 50.7 %shard_map.64.sol = bf16[8,625,256]{2,1,0:T(8,128)(2,1)S(1)} custom-call(s32[8]{0:T(128)} %bitcast.14, s32[3,1,8]{2,1,0:T(1,128)} %bitcast.19, bf16[8,128,128]{2,1,0:T(8,128)(2,1)} %constant.2.clone.table_hbm, bf16[375,625]{1,0:T(8,128)(2,1)} %bitcast.18, bf16[625,8,256]{2,1,0:T(8,128)(2,1)} %bitcast.17, bf16[625,8,625]{2,1,0:T(8,128)(2,1)} %bitcast.16), custom_call_target="tpu_custom_call" | custom-call | tf_op jit(solution)/shard_map/pallas_call | solution.py:323
  50.7 0.0 copy-done
  50.7 3.0 %shard_map.65 = bf16[625,8,256]{2,1,0:T(8,128)(2,1)} custom-call(s32[8]{0:T(128)S(1)} %bitcast.15, bf16[8,625,256]{2,1,0:T(8,128)(2,1)S(1)} %shard_map.64.sol), custom_call_target="tpu_custom_call" | custom-call | tf_op jit(solution)/shard_map/pallas_call | solution.py:357
Async XLA Ops:
  0.0 50.7 %copy-start = (s32[1,1,8]{2,1,0:T(1,128)S(1)}, s32[1,1,8]{2,1,0:T(1,128)}, u32[]{:S(2)}) copy-start(s32[1,1,8]{2,1,0:T(1,128)} %param.9) | copy-start | bytes 100
where the time goes:
time: 53.9 us; the launch traced here: 53.7 us
  Pallas kernels  53.7 us (100%)
    pallas_call x1, Pallas kernels, on_device(): pl.pallas_call(sweep_kernel, out_shape=pltpu.VMEM((planes, block, columns...  50.7 us
    pallas_call x1, Pallas kernels, on_device(): pl.pallas_call(place_kernel, out_shape=jax.ShapeDtypeStruct(rhs.shape, bf...  3 us

commit v1 on v0

--- a/solution.py
+++ b/solution.py
@@ -14,7 +14,6 @@
 FACE = VARS * SQUARE
 BLOCK = FACE * NODES
 LANE = 128
-CHUNKS = 1
 MESH = pl.DeviceIdType.MESH
 
 
@@ -44,11 +43,11 @@
 
 def sweep_kernel(
     order, orient, table_hbm, lift_hbm, rhs_hbm, inv_hbm, sol,
-    table, lift, raw_r, raw_b, stage, rhs, inv, padded, turned, wide, part, picked, trace_m, trace_r,
+    table, lift, raw_r, raw_b, stage, rhs, inv, padded, turned, plain, wide, weight, part, trace_m, trace_r,
     inc, out, load_sem, r_sem, b_sem, x_send, y_send, x_recv, y_recv,
 ):
     planes, block, columns = rhs.shape
-    width = columns // CHUNKS
+    parts = columns // LANE
     two, three = 2 * LANE, 3 * LANE
     chunks = row_chunks(block)
     tiles = [(t, min(LANE, block - t)) for t in range(0, block, LANE)]
@@ -61,8 +60,7 @@
         pltpu.make_async_copy(source, target, load_sem.at[i])
         for i, (source, target) in enumerate([(lift_hbm, lift), (table_hbm, table)])
     ]
-    for load in loads:
-        load.start()
+    loads[0].start()
 
     def fetch(i, start, size):
         rows = pl.ds(start, size)
@@ -71,11 +69,10 @@
             pltpu.make_async_copy(inv_hbm.at[rows], raw_b.at[rows], b_sem.at[i]),
         )
 
-    whole = block // LANE
-    depth = min(2, len(chunks))
-    for i, (start, size) in list(enumerate(chunks))[:depth]:
+    for i, (start, size) in enumerate(chunks):
         for copy in fetch(i, start, size):
             copy.start()
+    loads[1].start()
 
     barrier = pltpu.get_barrier_semaphore()
     for present, x, y in (
@@ -90,14 +87,17 @@
 
     part[...] = jnp.zeros_like(part)
     out[0] = jnp.zeros(out.shape[1:], out.dtype)
+    for d in range(3):
+        tail = (d + 1) * LANE - 8
+        trace_r[:, :, tail : tail + 8, :] = jnp.zeros((planes, parts, 8, LANE), trace_r.dtype)
 
     @pl.when(me_x == 0)
     def _():
-        inc[:, :, :LANE, :] = jnp.zeros((planes, CHUNKS, LANE, width), inc.dtype)
+        inc[:, :, :LANE, :] = jnp.zeros((planes, parts, LANE, LANE), inc.dtype)
 
     @pl.when(me_y == 0)
     def _():
-        inc[:, :, LANE:, :] = jnp.zeros((planes, CHUNKS, LANE, width), inc.dtype)
+        inc[:, :, LANE:, :] = jnp.zeros((planes, parts, LANE, LANE), inc.dtype)
 
     row = lax.broadcasted_iota(jnp.int32, (3 * FACE, three), 0)
     col = lax.broadcasted_iota(jnp.int32, (3 * FACE, three), 1)
@@ -108,7 +108,8 @@
     padded[...] = lax.dot_general(
         lift[...], spread, (((0,), (0,)), ((), ())), preferred_element_type=jnp.float32
     ).astype(jnp.bfloat16)
-    loads[1].wait()
+
+    whole = block // LANE
 
     def split(raw, into, rows, size, lanes, t):
         mixed = raw[rows, :, lanes].astype(jnp.float32)
@@ -121,18 +122,6 @@
     def arrange(i, start, size):
         for copy in fetch(i, start, size):
             copy.wait()
-        if size == LANE:
-            @pl.when(i + depth < whole)
-            def _():
-                for copy in fetch(i + depth, pl.multiple_of(start + depth * LANE, LANE), LANE):
-                    copy.start()
-
-            if whole < len(chunks):
-                @pl.when(i + depth == whole)
-                def _():
-                    for copy in fetch(whole, *chunks[whole]):
-                        copy.start()
-
         rows = pl.ds(start, size)
         for t, (first, wide_lanes) in enumerate(tiles):
             split(raw_b, inv, rows, size, slice(first, first + wide_lanes), t)
@@ -146,6 +135,7 @@
     lax.fori_loop(0, whole, arrange_full, 0)
     for i, (start, size) in list(enumerate(chunks))[whole:]:
         arrange(i, start, size)
+    loads[1].wait()
 
     def pick(source, put):
         for v in range(VARS):
@@ -156,21 +146,25 @@
 
     def prepare(k):
         slot = order[k]
-        for t, (first, wide_lanes) in enumerate(tiles):
-            wide[t, :, :wide_lanes] = inv[slot, :, first : first + wide_lanes].astype(jnp.float32)
-
-            def put(start, rows):
-                part[t, pl.ds(start, rows.shape[0]), :] = rows
-
-            pick(wide.at[t], put)
-            picked[:, first : first + wide_lanes] = part[t, :, :wide_lanes].astype(jnp.bfloat16)
-        moved = dot(picked[...], padded[...]).astype(jnp.bfloat16)
+        solved = dot(inv[slot], rhs[slot])
+        for c in range(parts):
+            plain[k, c] = solved[:, c * LANE : (c + 1) * LANE]
+
+            def put_plain(start, rows):
+                trace_r[k, c, pl.ds(start, rows.shape[0]), :] = rows
+
+            pick(plain.at[k, c], put_plain)
+        spreads = dot(inv[slot], padded[...])
+        weight[k] = spreads.astype(jnp.bfloat16)
         for d in range(3):
-            tile = slice(d * LANE, (d + 1) * LANE)
-            trace_m[k, :, tile] = dot(moved[:, tile], table[orient[d, 0, slot]]).astype(jnp.bfloat16)
-        plain = dot(picked[...], rhs[slot])
-        for c in range(CHUNKS):
-            trace_r[k, c] = plain[:, c * width : (c + 1) * width]
+            wide[d] = spreads[:, d * LANE : (d + 1) * LANE]
+
+            def put_part(start, rows):
+                part[d, pl.ds(start, rows.shape[0]), :] = rows
+
+            pick(wide.at[d], put_part)
+            moved = dot(part[d].astype(jnp.bfloat16), table[orient[d, 0, slot]])
+            trace_m[k, :, d * LANE : (d + 1) * LANE] = moved.astype(jnp.bfloat16)
 
     def hop(k, c, axis):
         rows = pl.ds(axis * LANE, LANE)
@@ -213,14 +207,14 @@
 
     def finish(k):
         slot = order[k]
-        faces = [[inc[k, c, d * LANE : (d + 1) * LANE, :] for c in range(CHUNKS)] for d in range(2)]
-        faces.append([out[k, c, two:, :] for c in range(CHUNKS)])
+        faces = [[inc[k, c, d * LANE : (d + 1) * LANE, :] for c in range(parts)] for d in range(2)]
+        faces.append([out[k, c, two:, :] for c in range(parts)])
         for d in range(3):
             face = jnp.concatenate(faces[d], axis=-1)
             turned[d * LANE : (d + 1) * LANE, :] = dot(table[orient[d, 0, slot]], face).astype(jnp.bfloat16)
-        lifted = dot(padded[...], turned[...])
-        source = (rhs[slot].astype(jnp.float32) - lifted).astype(jnp.bfloat16)
-        sol[k] = dot(inv[slot], source).astype(jnp.bfloat16)
+        lifted = dot(weight[k], turned[...])
+        for c in range(parts):
+            sol[c, pl.ds(k, block, stride=planes), :] = plain[k, c] - lifted[:, c * LANE : (c + 1) * LANE]
 
     distance = me_x + me_y
     lead = jnp.minimum(1 + 2 * distance, planes)
@@ -236,7 +230,7 @@
     pl.semaphore_wait(barrier, neighbours)
 
     def step(k, carry):
-        for c in range(CHUNKS):
+        for c in range(parts):
             advance(k, c)
 
         @pl.when(k + lead < planes)
@@ -260,7 +254,7 @@
         lax.fori_loop(0, planes, late, 0)
 
     def drain(k, carry):
-        for c in range(CHUNKS):
+        for c in range(parts):
             @pl.when(has_right)
             def _():
                 hop(k, c, 0).wait_send()
@@ -273,10 +267,14 @@
     lax.fori_loop(0, planes, drain, 0)
 
 
-def place_kernel(order, sol, out, stage, ready, sems):
-    planes, block, columns = sol.shape
+def place_kernel(order, sol, out, ready, sems):
+    block, planes, columns = ready.shape
     chunks = row_chunks(block)
     whole = block // LANE
+    place_of = lax.broadcasted_iota(jnp.int32, (planes, LANE), 0)
+    source = jnp.zeros((planes, LANE), jnp.int32)
+    for k in range(planes):
+        source = jnp.where(place_of == order[k], k, source)
 
     def put(i, start, size):
         rows = pl.ds(start, size)
@@ -284,13 +282,12 @@
 
     def place(i, start, size):
         rows = pl.ds(start, size)
+        picks = jnp.broadcast_to(source[None], (size, planes, LANE))
         for t in range(columns // LANE):
             lanes = slice(t * LANE, (t + 1) * LANE)
-            for k in range(planes):
-                stage[t, pl.ds(order[k], size, stride=planes), :] = sol[k, rows, lanes].astype(jnp.float32)
-            ready[rows, :, lanes] = (
-                stage[t, : size * planes, :].reshape(size, planes, LANE).astype(jnp.bfloat16)
-            )
+            swept = sol[t, pl.ds(start * planes, size * planes), :].reshape(size, planes, LANE)
+            placed = jnp.take_along_axis(swept, picks, axis=1, mode="promise_in_bounds")
+            ready[rows, :, lanes] = placed.astype(jnp.bfloat16)
         put(i, start, size).start()
 
     def place_full(i, carry):
@@ -312,7 +309,7 @@
     block, planes, columns = rhs.shape
     tiles = pl.cdiv(block, LANE)
     chunks = len(row_chunks(block))
-    width = columns // CHUNKS
+    parts = columns // LANE
     two, three = 2 * LANE, 3 * LANE
     bf16, f32 = jnp.bfloat16, jnp.float32
     table = jnp.asarray(orient_table(), bf16)
@@ -322,7 +319,7 @@
     anywhere = pl.BlockSpec(memory_space=pl.ANY)
     sol = pl.pallas_call(
         sweep_kernel,
-        out_shape=pltpu.VMEM((planes, block, columns), bf16),
+        out_shape=pltpu.VMEM((parts, block * planes, LANE), f32),
         in_specs=[smem, smem] + [anywhere] * 4,
         out_specs=vmem,
         scratch_shapes=[
@@ -335,23 +332,24 @@
             pltpu.VMEM((planes, block, block), bf16),
             pltpu.VMEM((block, three), bf16),
             pltpu.VMEM((three, columns), bf16),
-            pltpu.VMEM((tiles, block, LANE), f32),
-            pltpu.VMEM((tiles, three, LANE), f32),
-            pltpu.VMEM((three, block), bf16),
+            pltpu.VMEM((planes, parts, block, LANE), f32),
+            pltpu.VMEM((3, block, LANE), f32),
+            pltpu.VMEM((planes, block, three), bf16),
+            pltpu.VMEM((3, three, LANE), f32),
             pltpu.VMEM((planes, three, three), bf16),
-            pltpu.VMEM((planes, CHUNKS, three, width), f32),
-            pltpu.VMEM((planes, CHUNKS, two, width), bf16),
-            pltpu.VMEM((planes + 1, CHUNKS, three, width), bf16),
+            pltpu.VMEM((planes, parts, three, LANE), f32),
+            pltpu.VMEM((planes, parts, two, LANE), bf16),
+            pltpu.VMEM((planes + 1, parts, three, LANE), bf16),
             pltpu.SemaphoreType.DMA((2,)),
             pltpu.SemaphoreType.DMA((chunks,)),
             pltpu.SemaphoreType.DMA((chunks,)),
-            pltpu.SemaphoreType.DMA((planes, CHUNKS)),
-            pltpu.SemaphoreType.DMA((planes, CHUNKS)),
-            pltpu.SemaphoreType.DMA((planes, CHUNKS)),
-            pltpu.SemaphoreType.DMA((planes, CHUNKS)),
+            pltpu.SemaphoreType.DMA((planes, parts)),
+            pltpu.SemaphoreType.DMA((planes, parts)),
+            pltpu.SemaphoreType.DMA((planes, parts)),
+            pltpu.SemaphoreType.DMA((planes, parts)),
         ],
         compiler_params=pltpu.CompilerParams(
-            collective_id=0, has_side_effects=True, vmem_limit_bytes=60 * 1024 * 1024
+            collective_id=0, has_side_effects=True, vmem_limit_bytes=54 * 1024 * 1024
         ),
     )(order, orient, table, lift, rhs, inv)
     result = pl.pallas_call(
@@ -360,7 +358,6 @@
         in_specs=[smem, vmem],
         out_specs=anywhere,
         scratch_shapes=[
-            pltpu.VMEM((columns // LANE, LANE * planes, LANE), f32),
             pltpu.VMEM(rhs.shape, bf16),
             pltpu.SemaphoreType.DMA((chunks,)),
         ],

time: 53.9 us -> 55.8 us (1.035)
  Pallas kernels: 53.7 us -> 55.7 us
    pallas_call x1, Pallas kernels: 50.7 us -> 53.5 us  [on_device(): pl.pallas_call(sweep_kernel, out_shape=pltpu.VMEM((parts, block * planes,...]
    pallas_call x1, Pallas kernels: 3 us -> 2.13 us  [on_device(): pl.pallas_call(place_kernel, out_shape=jax.ShapeDtypeStruct(rhs.shape, bf...]
where the time goes in v1:
time: 55.8 us; the launch traced here: 55.7 us
  Pallas kernels  55.7 us (100%)
    pallas_call x1, Pallas kernels, on_device(): pl.pallas_call(sweep_kernel, out_shape=pltpu.VMEM((parts, block * planes,...  53.5 us
    pallas_call x1, Pallas kernels, on_device(): pl.pallas_call(place_kernel, out_shape=jax.ShapeDtypeStruct(rhs.shape, bf...  2.13 us

profile of v1, /device:TPU:31, one launch (start us, length us, event | category | flops | bytes accessed | tf_op | source)
XLA Modules:
  0.0 55.7 jit_solution(10571533005341848392)
XLA Ops:
  0.0 0.0 copy-start
  0.0 53.5 %shard_map.64.sol = f32[2,5000,128]{2,1,0:T(8,128)S(1)} custom-call(s32[8]{0:T(128)} %bitcast.14, s32[3,1,8]{2,1,0:T(1,128)} %bitcast.19, bf16[8,128,128]{2,1,0:T(8,128)(2,1)} %constant.2.clone.table_hbm, bf16[375,625]{1,0:T(8,128)(2,1)} %bitcast.18, bf16[625,8,256]{2,1,0:T(8,128)(2,1)} %bitcast.17, bf16[625,8,625]{2,1,0:T(8,128)(2,1)} %bitcast.16), custom_call_target="tpu_custom_call" | custom-call | tf_op jit(solution)/shard_map/pallas_call | solution.py:320
  53.6 0.0 copy-done
  53.6 2.1 %shard_map.65 = bf16[625,8,256]{2,1,0:T(8,128)(2,1)} custom-call(s32[8]{0:T(128)S(1)} %bitcast.15, f32[2,5000,128]{2,1,0:T(8,128)S(1)} %shard_map.64.sol), custom_call_target="tpu_custom_call" | custom-call | tf_op jit(solution)/shard_map/pallas_call | solution.py:355
Async XLA Ops:
  0.0 53.6 %copy-start = (s32[1,1,8]{2,1,0:T(1,128)S(1)}, s32[1,1,8]{2,1,0:T(1,128)}, u32[]{:S(2)}) copy-start(s32[1,1,8]{2,1,0:T(1,128)} %param.9) | copy-start | bytes 100

commit v2 on v1

--- a/solution.py
+++ b/solution.py
@@ -43,10 +43,10 @@
 
 def sweep_kernel(
     order, orient, table_hbm, lift_hbm, rhs_hbm, inv_hbm, sol,
-    table, lift, raw_r, raw_b, stage, rhs, inv, padded, turned, plain, wide, weight, part, trace_m, trace_r,
-    inc, out, load_sem, r_sem, b_sem, x_send, y_send, x_recv, y_recv,
+    table, lift, raw_r, raw_b, stage, rhs, inv, padded, turned, plain, wide, weight, part, picked, trace_m, trace_r,
+    begun, inc, out, load_sem, r_sem, b_sem, x_send, y_send, x_recv, y_recv,
 ):
-    planes, block, columns = rhs.shape
+    block, planes, columns = raw_r.shape
     parts = columns // LANE
     two, three = 2 * LANE, 3 * LANE
     chunks = row_chunks(block)
@@ -69,7 +69,9 @@
             pltpu.make_async_copy(inv_hbm.at[rows], raw_b.at[rows], b_sem.at[i]),
         )
 
-    for i, (start, size) in enumerate(chunks):
+    whole = block // LANE
+    depth = min(2, len(chunks))
+    for i, (start, size) in list(enumerate(chunks))[:depth]:
         for copy in fetch(i, start, size):
             copy.start()
     loads[1].start()
@@ -91,6 +93,12 @@
         tail = (d + 1) * LANE - 8
         trace_r[:, :, tail : tail + 8, :] = jnp.zeros((planes, parts, 8, LANE), trace_r.dtype)
 
+    distance = me_x + me_y
+
+    @pl.when(distance == 0)
+    def _():
+        trace_m[:, :, :two] = jnp.zeros((planes, three, two), trace_m.dtype)
+
     @pl.when(me_x == 0)
     def _():
         inc[:, :, :LANE, :] = jnp.zeros((planes, parts, LANE, LANE), inc.dtype)
@@ -109,24 +117,30 @@
         lift[...], spread, (((0,), (0,)), ((), ())), preferred_element_type=jnp.float32
     ).astype(jnp.bfloat16)
 
-    whole = block // LANE
-
-    def split(raw, into, rows, size, lanes, t):
-        mixed = raw[rows, :, lanes].astype(jnp.float32)
-        wide_lanes = mixed.shape[-1]
-        stage[t, : size * planes, :wide_lanes] = mixed.reshape(size * planes, wide_lanes)
-        for s in range(planes):
-            apart = stage[t, pl.ds(s, size, stride=planes), :]
-            into[s, rows, lanes] = apart[:, :wide_lanes].astype(jnp.bfloat16)
+    def widen(raw, start, size, lanes, t):
+        mixed = raw[pl.ds(start, size), :, lanes].astype(jnp.float32)
+        rows = pl.ds(start * planes, size * planes)
+        stage[t, rows, : mixed.shape[-1]] = mixed.reshape(size * planes, mixed.shape[-1])
 
     def arrange(i, start, size):
         for copy in fetch(i, start, size):
             copy.wait()
-        rows = pl.ds(start, size)
-        for t, (first, wide_lanes) in enumerate(tiles):
-            split(raw_b, inv, rows, size, slice(first, first + wide_lanes), t)
+        if size == LANE:
+            @pl.when(i + depth < whole)
+            def _():
+                for copy in fetch(i + depth, pl.multiple_of(start + depth * LANE, LANE), LANE):
+                    copy.start()
+
+            if whole < len(chunks):
+                @pl.when(i + depth == whole)
+                def _():
+                    for copy in fetch(whole, *chunks[whole]):
+                        copy.start()
+
+        for t, (first, lanes) in enumerate(tiles):
+            widen(raw_b, start, size, slice(first, first + lanes), t)
         for t in range(columns // LANE):
-            split(raw_r, rhs, rows, size, slice(t * LANE, (t + 1) * LANE), len(tiles) + t)
+            widen(raw_r, start, size, slice(t * LANE, (t + 1) * LANE), len(tiles) + t)
 
     def arrange_full(i, carry):
         arrange(i, pl.multiple_of(i * LANE, LANE), LANE)
@@ -137,34 +151,68 @@
         arrange(i, start, size)
     loads[1].wait()
 
-    def pick(source, put):
+    def pick(source, put, first, step):
+        def rows(start, size, stride=1):
+            return source[pl.ds(first + start * step, size, stride=stride * step), :]
+
         for v in range(VARS):
-            put(v * SQUARE, source[pl.ds(v * FACE + FACE - SQUARE, SQUARE), :])
+            put(v * SQUARE, rows(v * FACE + FACE - SQUARE, SQUARE))
         for v in range(VARS * NODES):
-            put(LANE + v * NODES, source[pl.ds(v * SQUARE + SQUARE - NODES, NODES), :])
-        put(two, source[pl.ds(NODES - 1, FACE, stride=NODES), :])
-
-    def prepare(k):
+            put(LANE + v * NODES, rows(v * SQUARE + SQUARE - NODES, NODES))
+        put(two, rows(NODES - 1, FACE, NODES))
+
+    def take_right(slot, into=0):
+        for t in range(parts):
+            rows = stage[len(tiles) + t, pl.ds(slot, block, stride=planes), :]
+            rhs[into, :, t * LANE : (t + 1) * LANE] = rows.astype(jnp.bfloat16)
+
+    def take_block(slot):
+        for t, (first, lanes) in enumerate(tiles):
+            rows = stage[t, pl.ds(slot, block, stride=planes), :]
+            inv[:, first : first + lanes] = rows[:, :lanes].astype(jnp.bfloat16)
+
+    def turn_into(k, d, moved, slot):
+        turned_face = dot(moved.astype(jnp.bfloat16), table[orient[d, 0, slot]])
+        trace_m[k, :, d * LANE : (d + 1) * LANE] = turned_face.astype(jnp.bfloat16)
+
+    def prepare_traces(k, first_face, u=0):
         slot = order[k]
-        solved = dot(inv[slot], rhs[slot])
+        for t, (first, lanes) in enumerate(tiles):
+            def put_part(start, rows):
+                part[u, t, pl.ds(start, rows.shape[0]), :] = rows
+
+            pick(stage.at[t], put_part, slot, planes)
+            picked[u, :, first : first + lanes] = part[u, t, :, :lanes].astype(jnp.bfloat16)
+        take_right(slot, u)
+        solved = dot(picked[u], rhs[u])
+        for c in range(parts):
+            trace_r[k, c] = solved[:, c * LANE : (c + 1) * LANE]
+        moved = dot(picked[u], padded[:, first_face * LANE :])
+        for d in range(first_face, 3):
+            turn_into(k, d, moved[:, (d - first_face) * LANE : (d - first_face + 1) * LANE], slot)
+
+    def prepare_all(k):
+        slot = order[k]
+        take_right(slot)
+        take_block(slot)
+        solved = dot(inv[...], rhs[0])
         for c in range(parts):
             plain[k, c] = solved[:, c * LANE : (c + 1) * LANE]
 
             def put_plain(start, rows):
                 trace_r[k, c, pl.ds(start, rows.shape[0]), :] = rows
 
-            pick(plain.at[k, c], put_plain)
-        spreads = dot(inv[slot], padded[...])
+            pick(plain.at[k, c], put_plain, 0, 1)
+        spreads = dot(inv[...], padded[...])
         weight[k] = spreads.astype(jnp.bfloat16)
         for d in range(3):
             wide[d] = spreads[:, d * LANE : (d + 1) * LANE]
 
             def put_part(start, rows):
-                part[d, pl.ds(start, rows.shape[0]), :] = rows
-
-            pick(wide.at[d], put_part)
-            moved = dot(part[d].astype(jnp.bfloat16), table[orient[d, 0, slot]])
-            trace_m[k, :, d * LANE : (d + 1) * LANE] = moved.astype(jnp.bfloat16)
+                part[0, d, pl.ds(start, rows.shape[0]), :] = rows
+
+            pick(wide.at[d], put_part, 0, 1)
+            turn_into(k, d, part[0, d], slot)
 
     def hop(k, c, axis):
         rows = pl.ds(axis * LANE, LANE)
@@ -179,8 +227,6 @@
         )
 
     def advance(k, c):
-        started = trace_r[k, c] - dot(trace_m[k, :, two:], out[k, c, two:, :])
-
         @pl.when(has_left)
         def _():
             hop(k, c, 0).wait_recv()
@@ -189,69 +235,115 @@
         def _():
             hop(k, c, 1).wait_recv()
 
-        arrived = inc[k, c]
-        ahead_rows = (started[:two] - dot(trace_m[k, :two, :two], arrived)).astype(jnp.bfloat16)
-        out[k + 1, c, LANE:two, :] = ahead_rows[LANE:]
+        gone = dot(trace_m[k, :two, :two], inc[k, c])
+        out[k + 1, c, :two, :] = (begun[c, :two, :] - gone).astype(jnp.bfloat16)
 
         @pl.when(has_above)
         def _():
             hop(k, c, 1).start()
 
-        out[k + 1, c, :LANE, :] = ahead_rows[:LANE]
-
         @pl.when(has_right)
         def _():
             hop(k, c, 0).start()
 
-        out[k + 1, c, two:, :] = (started[two:] - dot(trace_m[k, two:, :two], arrived)).astype(jnp.bfloat16)
-
-    def finish(k):
-        slot = order[k]
+    def follow(k):
+        arrived = jnp.concatenate([inc[k, c] for c in range(parts)], axis=-1)
+        gone = dot(trace_m[k, two:, :two], arrived)
+        rising = [
+            (begun[c, two:, :] - gone[:, c * LANE : (c + 1) * LANE]).astype(jnp.bfloat16) for c in range(parts)
+        ]
+        later = jnp.minimum(k + 1, planes - 1)
+        lifted = dot(trace_m[later, :, two:], jnp.concatenate(rising, axis=-1))
+        for c in range(parts):
+            out[k + 1, c, two:, :] = rising[c]
+            begun[c] = trace_r[later, c] - lifted[:, c * LANE : (c + 1) * LANE]
+
+    def turn_faces(k, slot):
         faces = [[inc[k, c, d * LANE : (d + 1) * LANE, :] for c in range(parts)] for d in range(2)]
         faces.append([out[k, c, two:, :] for c in range(parts)])
         for d in range(3):
             face = jnp.concatenate(faces[d], axis=-1)
             turned[d * LANE : (d + 1) * LANE, :] = dot(table[orient[d, 0, slot]], face).astype(jnp.bfloat16)
+
+    def finish_late(k):
+        slot = order[k]
+        take_block(slot)
+        turn_faces(k, slot)
+        lifted = dot(padded[...], turned[...])
+        for t in range(parts):
+            rows = stage[len(tiles) + t, pl.ds(slot, block, stride=planes), :]
+            rhs[0, :, t * LANE : (t + 1) * LANE] = (rows - lifted[:, t * LANE : (t + 1) * LANE]).astype(jnp.bfloat16)
+        swept = dot(inv[...], rhs[0])
+        for c in range(parts):
+            sol[c, pl.ds(k, block, stride=planes), :] = swept[:, c * LANE : (c + 1) * LANE]
+
+    def finish(k):
+        turn_faces(k, order[k])
         lifted = dot(weight[k], turned[...])
         for c in range(parts):
             sol[c, pl.ds(k, block, stride=planes), :] = plain[k, c] - lifted[:, c * LANE : (c + 1) * LANE]
 
-    distance = me_x + me_y
-    lead = jnp.minimum(1 + 2 * distance, planes)
-    near = distance * 2 <= count_x + count_y - 2
-
-    def ahead(k, carry):
-        prepare(k)
-        return carry
-
-    lax.fori_loop(0, lead, ahead, 0)
-
+    near = distance * 5 <= (count_x + count_y - 2) * 2
     neighbours = sum(p.astype(jnp.int32) for p in (has_left, has_right, has_below, has_above))
-    pl.semaphore_wait(barrier, neighbours)
-
-    def step(k, carry):
+
+    def loop(start, stop, *works):
+        def body(k, carry):
+            for work in works:
+                work(k)
+            return carry
+
+        lax.fori_loop(start, stop, body, 0)
+
+    def advances(k):
         for c in range(parts):
             advance(k, c)
 
-        @pl.when(k + lead < planes)
-        def _():
-            prepare(k + lead)
-
-        @pl.when(jnp.logical_not(near))
-        def _():
-            finish(k)
-
-        return carry
-
-    lax.fori_loop(0, planes, step, 0)
+    def enter():
+        pl.semaphore_wait(barrier, neighbours)
+        begun[...] = trace_r[0]
+
+    def prepare_pair(k):
+        for u in range(2):
+            prepare_traces(2 * k + u, 0, u)
+
+    @pl.when(distance == 0)
+    def _():
+        prepare_traces(0, 2)
+        enter()
+        loop(0, planes - 1, advances, lambda k: prepare_traces(k + 1, 2), follow)
+        loop(planes - 1, planes, advances, follow)
+
+    early = (distance > 0) & (distance * 10 <= (count_x + count_y - 2) * 3)
+
+    @pl.when(early)
+    def _():
+        loop(0, planes // 4, prepare_pair)
+        enter()
+
+        def two_steps(j):
+            advances(2 * j)
+            prepare_traces(2 * (planes // 4) + j, 0)
+            follow(2 * j)
+            advances(2 * j + 1)
+            follow(2 * j + 1)
+
+        loop(0, planes // 2, two_steps)
+
+    @pl.when(near & (distance > 0) & jnp.logical_not(early))
+    def _():
+        loop(0, planes // 2, prepare_pair)
+        enter()
+        loop(0, planes, advances, follow)
 
     @pl.when(near)
     def _():
-        def late(k, carry):
-            finish(k)
-            return carry
-
-        lax.fori_loop(0, planes, late, 0)
+        loop(0, planes, finish_late)
+
+    @pl.when(jnp.logical_not(near))
+    def _():
+        loop(0, planes, prepare_all)
+        enter()
+        loop(0, planes, advances, follow, finish)
 
     def drain(k, carry):
         for c in range(parts):
@@ -327,17 +419,19 @@
             pltpu.VMEM(lift.shape, bf16),
             pltpu.VMEM(rhs.shape, bf16),
             pltpu.VMEM(inv.shape, bf16),
-            pltpu.VMEM((tiles + columns // LANE, LANE * planes, LANE), f32),
-            pltpu.VMEM((planes, block, columns), bf16),
-            pltpu.VMEM((planes, block, block), bf16),
+            pltpu.VMEM((tiles + parts, block * planes, LANE), f32),
+            pltpu.VMEM((2, block, columns), bf16),
+            pltpu.VMEM((block, block), bf16),
             pltpu.VMEM((block, three), bf16),
             pltpu.VMEM((three, columns), bf16),
             pltpu.VMEM((planes, parts, block, LANE), f32),
             pltpu.VMEM((3, block, LANE), f32),
             pltpu.VMEM((planes, block, three), bf16),
-            pltpu.VMEM((3, three, LANE), f32),
+            pltpu.VMEM((2, max(tiles, 3), three, LANE), f32),
+            pltpu.VMEM((2, three, block), bf16),
             pltpu.VMEM((planes, three, three), bf16),
             pltpu.VMEM((planes, parts, three, LANE), f32),
+            pltpu.VMEM((parts, three, LANE), f32),
             pltpu.VMEM((planes, parts, two, LANE), bf16),
             pltpu.VMEM((planes + 1, parts, three, LANE), bf16),
             pltpu.SemaphoreType.DMA((2,)),
@@ -349,7 +443,7 @@
             pltpu.SemaphoreType.DMA((planes, parts)),
         ],
         compiler_params=pltpu.CompilerParams(
-            collective_id=0, has_side_effects=True, vmem_limit_bytes=54 * 1024 * 1024
+            collective_id=0, has_side_effects=True, vmem_limit_bytes=57 * 1024 * 1024
         ),
     )(order, orient, table, lift, rhs, inv)
     result = pl.pallas_call(

time: 55.8 us -> 50.1 us (0.90)
  Pallas kernels: 55.7 us -> 49.8 us
    pallas_call x1, Pallas kernels: 53.5 us -> 47.7 us  [on_device(): pl.pallas_call(sweep_kernel, out_shape=pltpu.VMEM((parts, block * planes,...]
where the time goes in v2:
time: 50.1 us; the launch traced here: 50 us
  Pallas kernels  49.8 us (99%)
    pallas_call x1, Pallas kernels, on_device(): pl.pallas_call(sweep_kernel, out_shape=pltpu.VMEM((parts, block * planes,...  47.7 us
    pallas_call x1, Pallas kernels, on_device(): pl.pallas_call(place_kernel, out_shape=jax.ShapeDtypeStruct(rhs.shape, bf...  2.13 us

profile of v2, /device:TPU:31, one launch (start us, length us, event | category | flops | bytes accessed | tf_op | source)
XLA Modules:
  0.0 50.0 jit_solution(9776518728162612385)
XLA Ops:
  0.0 0.0 copy-start
  0.0 47.7 %shard_map.64.sol = f32[2,5000,128]{2,1,0:T(8,128)S(1)} custom-call(s32[8]{0:T(128)} %bitcast.14, s32[3,1,8]{2,1,0:T(1,128)} %bitcast.19, bf16[8,128,128]{2,1,0:T(8,128)(2,1)} %constant.2.clone.table_hbm, bf16[375,625]{1,0:T(8,128)(2,1)} %bitcast.18, bf16[625,8,256]{2,1,0:T(8,128)(2,1)} %bitcast.17, bf16[625,8,625]{2,1,0:T(8,128)(2,1)} %bitcast.16), custom_call_target="tpu_custom_call" | custom-call | tf_op jit(solution)/shard_map/pallas_call | solution.py:412
  47.7 0.0 copy-done
  47.7 2.1 %shard_map.65 = bf16[625,8,256]{2,1,0:T(8,128)(2,1)} custom-call(s32[8]{0:T(128)S(1)} %bitcast.15, f32[2,5000,128]{2,1,0:T(8,128)S(1)} %shard_map.64.sol), custom_call_target="tpu_custom_call" | custom-call | tf_op jit(solution)/shard_map/pallas_call | solution.py:449
Async XLA Ops:
  0.0 47.7 %copy-start = (s32[1,1,8]{2,1,0:T(1,128)S(1)}, s32[1,1,8]{2,1,0:T(1,128)}, u32[]{:S(2)}) copy-start(s32[1,1,8]{2,1,0:T(1,128)} %param.9) | copy-start | bytes 100

commit v3 on v2

--- a/solution.py
+++ b/solution.py
@@ -70,7 +70,7 @@
         )
 
     whole = block // LANE
-    depth = min(2, len(chunks))
+    depth = min(3, len(chunks))
     for i, (start, size) in list(enumerate(chunks))[:depth]:
         for copy in fetch(i, start, size):
             copy.start()
@@ -95,10 +95,6 @@
 
     distance = me_x + me_y
 
-    @pl.when(distance == 0)
-    def _():
-        trace_m[:, :, :two] = jnp.zeros((planes, three, two), trace_m.dtype)
-
     @pl.when(me_x == 0)
     def _():
         inc[:, :, :LANE, :] = jnp.zeros((planes, parts, LANE, LANE), inc.dtype)
@@ -175,7 +171,7 @@
         turned_face = dot(moved.astype(jnp.bfloat16), table[orient[d, 0, slot]])
         trace_m[k, :, d * LANE : (d + 1) * LANE] = turned_face.astype(jnp.bfloat16)
 
-    def prepare_traces(k, first_face, u=0):
+    def gather(k, u=0):
         slot = order[k]
         for t, (first, lanes) in enumerate(tiles):
             def put_part(start, rows):
@@ -184,6 +180,9 @@
             pick(stage.at[t], put_part, slot, planes)
             picked[u, :, first : first + lanes] = part[u, t, :, :lanes].astype(jnp.bfloat16)
         take_right(slot, u)
+
+    def solve(k, first_face, u=0):
+        slot = order[k]
         solved = dot(picked[u], rhs[u])
         for c in range(parts):
             trace_r[k, c] = solved[:, c * LANE : (c + 1) * LANE]
@@ -237,7 +236,9 @@
 
         gone = dot(trace_m[k, :two, :two], inc[k, c])
         out[k + 1, c, :two, :] = (begun[c, :two, :] - gone).astype(jnp.bfloat16)
-
+        send(k, c)
+
+    def send(k, c):
         @pl.when(has_above)
         def _():
             hop(k, c, 1).start()
@@ -256,6 +257,19 @@
         lifted = dot(trace_m[later, :, two:], jnp.concatenate(rising, axis=-1))
         for c in range(parts):
             out[k + 1, c, two:, :] = rising[c]
+            begun[c] = trace_r[later, c] - lifted[:, c * LANE : (c + 1) * LANE]
+
+    def corner_sends(k):
+        for c in range(parts):
+            out[k + 1, c] = begun[c].astype(jnp.bfloat16)
+        for c in range(parts):
+            send(k, c)
+
+    def corner_follow(k):
+        rising = jnp.concatenate([begun[c, two:, :] for c in range(parts)], axis=-1).astype(jnp.bfloat16)
+        later = jnp.minimum(k + 1, planes - 1)
+        lifted = dot(trace_m[later, :, two:], rising)
+        for c in range(parts):
             begun[c] = trace_r[later, c] - lifted[:, c * LANE : (c + 1) * LANE]
 
     def turn_faces(k, slot):
@@ -304,30 +318,51 @@
 
     def prepare_pair(k):
         for u in range(2):
-            prepare_traces(2 * k + u, 0, u)
+            gather(2 * k + u, u)
+            solve(2 * k + u, 0, u)
 
     @pl.when(distance == 0)
     def _():
-        prepare_traces(0, 2)
+        last = planes - 1
+        gather(0, 0)
+        solve(0, 2, 0)
         enter()
-        loop(0, planes - 1, advances, lambda k: prepare_traces(k + 1, 2), follow)
-        loop(planes - 1, planes, advances, follow)
+
+        def two_steps(j):
+            corner_sends(2 * j)
+
+            @pl.when(j == 0)
+            def _():
+                gather(1, 1)
+
+            solve(2 * j + 1, 2, 1)
+            gather(jnp.minimum(2 * j + 2, last), 0)
+            corner_follow(2 * j)
+            corner_sends(2 * j + 1)
+            solve(jnp.minimum(2 * j + 2, last), 2, 0)
+            gather(jnp.minimum(2 * j + 3, last), 1)
+            corner_follow(2 * j + 1)
+
+        loop(0, planes // 2, two_steps)
 
     early = (distance > 0) & (distance * 10 <= (count_x + count_y - 2) * 3)
 
     @pl.when(early)
     def _():
-        loop(0, planes // 4, prepare_pair)
+        half = planes // 2
+        loop(0, half // 2, prepare_pair)
+        gather(half)
         enter()
 
         def two_steps(j):
             advances(2 * j)
-            prepare_traces(2 * (planes // 4) + j, 0)
+            solve(half + j, 0)
             follow(2 * j)
             advances(2 * j + 1)
+            gather(jnp.minimum(half + 1 + j, planes - 1))
             follow(2 * j + 1)
 
-        loop(0, planes // 2, two_steps)
+        loop(0, half, two_steps)
 
     @pl.when(near & (distance > 0) & jnp.logical_not(early))
     def _():

time: 50.1 us -> 48.7 us (0.972)
  Pallas kernels: 49.8 us -> 48.6 us
    pallas_call x1, Pallas kernels: 47.7 us -> 46.5 us  [on_device(): pl.pallas_call(sweep_kernel, out_shape=pltpu.VMEM((parts, block * planes,...]
where the time goes in v3:
time: 48.7 us; the launch traced here: 48.8 us
  Pallas kernels  48.6 us (100%)
    pallas_call x1, Pallas kernels, on_device(): pl.pallas_call(sweep_kernel, out_shape=pltpu.VMEM((parts, block * planes,...  46.5 us
    pallas_call x1, Pallas kernels, on_device(): pl.pallas_call(place_kernel, out_shape=jax.ShapeDtypeStruct(rhs.shape, bf...  2.13 us

profile of v3, /device:TPU:31, one launch (start us, length us, event | category | flops | bytes accessed | tf_op | source)
XLA Modules:
  0.0 48.8 jit_solution(4436335866472478091)
XLA Ops:
  0.0 0.0 copy-start
  0.0 46.5 %shard_map.64.sol = f32[2,5000,128]{2,1,0:T(8,128)S(1)} custom-call(s32[8]{0:T(128)} %bitcast.14, s32[3,1,8]{2,1,0:T(1,128)} %bitcast.19, bf16[8,128,128]{2,1,0:T(8,128)(2,1)} %constant.2.clone.table_hbm, bf16[375,625]{1,0:T(8,128)(2,1)} %bitcast.18, bf16[625,8,256]{2,1,0:T(8,128)(2,1)} %bitcast.17, bf16[625,8,625]{2,1,0:T(8,128)(2,1)} %bitcast.16), custom_call_target="tpu_custom_call" | custom-call | tf_op jit(solution)/shard_map/pallas_call | solution.py:447
  46.5 0.0 copy-done
  46.5 2.1 %shard_map.65 = bf16[625,8,256]{2,1,0:T(8,128)(2,1)} custom-call(s32[8]{0:T(128)S(1)} %bitcast.15, f32[2,5000,128]{2,1,0:T(8,128)S(1)} %shard_map.64.sol), custom_call_target="tpu_custom_call" | custom-call | tf_op jit(solution)/shard_map/pallas_call | solution.py:484
Async XLA Ops:
  0.0 46.5 %copy-start = (s32[1,1,8]{2,1,0:T(1,128)S(1)}, s32[1,1,8]{2,1,0:T(1,128)}, u32[]{:S(2)}) copy-start(s32[1,1,8]{2,1,0:T(1,128)} %param.9) | copy-start | bytes 100

commit v4 on v3

--- a/solution.py
+++ b/solution.py
@@ -351,16 +351,23 @@
     def _():
         half = planes // 2
         loop(0, half // 2, prepare_pair)
-        gather(half)
         enter()
 
         def two_steps(j):
             advances(2 * j)
+
+            @pl.when(j == 0)
+            def _():
+                gather(half)
+
             solve(half + j, 0)
             follow(2 * j)
             advances(2 * j + 1)
-            gather(jnp.minimum(half + 1 + j, planes - 1))
             follow(2 * j + 1)
+
+            @pl.when(j < half - 1)
+            def _():
+                gather(half + 1 + j)
 
         loop(0, half, two_steps)
 

time: 48.7 us -> 49 us (level)
  no operation moved by 1% of the time
where the time goes in v4:
time: 49 us; the launch traced here: 48.9 us
  Pallas kernels  48.7 us (99%)
    pallas_call x1, Pallas kernels, on_device(): pl.pallas_call(sweep_kernel, out_shape=pltpu.VMEM((parts, block * planes,...  46.6 us
    pallas_call x1, Pallas kernels, on_device(): pl.pallas_call(place_kernel, out_shape=jax.ShapeDtypeStruct(rhs.shape, bf...  2.13 us

profile of v4, /device:TPU:31, one launch (start us, length us, event | category | flops | bytes accessed | tf_op | source)
XLA Modules:
  0.0 48.9 jit_solution(14087289585254419699)
XLA Ops:
  0.0 0.0 copy-start
  0.0 46.6 %shard_map.64.sol = f32[2,5000,128]{2,1,0:T(8,128)S(1)} custom-call(s32[8]{0:T(128)} %bitcast.14, s32[3,1,8]{2,1,0:T(1,128)} %bitcast.19, bf16[8,128,128]{2,1,0:T(8,128)(2,1)} %constant.2.clone.table_hbm, bf16[375,625]{1,0:T(8,128)(2,1)} %bitcast.18, bf16[625,8,256]{2,1,0:T(8,128)(2,1)} %bitcast.17, bf16[625,8,625]{2,1,0:T(8,128)(2,1)} %bitcast.16), custom_call_target="tpu_custom_call" | custom-call | tf_op jit(solution)/shard_map/pallas_call | solution.py:454
  46.6 0.0 copy-done
  46.6 2.1 %shard_map.65 = bf16[625,8,256]{2,1,0:T(8,128)(2,1)} custom-call(s32[8]{0:T(128)S(1)} %bitcast.15, f32[2,5000,128]{2,1,0:T(8,128)S(1)} %shard_map.64.sol), custom_call_target="tpu_custom_call" | custom-call | tf_op jit(solution)/shard_map/pallas_call | solution.py:491
Async XLA Ops:
  0.0 46.6 %copy-start = (s32[1,1,8]{2,1,0:T(1,128)S(1)}, s32[1,1,8]{2,1,0:T(1,128)}, u32[]{:S(2)}) copy-start(s32[1,1,8]{2,1,0:T(1,128)} %param.9) | copy-start | bytes 100
